TPU v7x, 32 devices: a whole 2x2x4 slice. The times are simulated.
32 devices in a mesh: batch: 4 (over y, x), rows: 8 (over z, core).
Axes of the slice: x: 2, y: 2, z: 4, core: 2. Of those that a mesh axis runs over, the one named last changes fastest.
Arguments:
- features: bfloat16 [256, 8, 16, 2048], P('batch', 'rows'), may hold values from -6 to 6
- w_reduce: bfloat16 [2048, 512], P('rows'), may hold values from -0.125 to 0.125
- w_spatial: bfloat16 [4608, 512], P('rows'), may hold values from -0.09375 to 0.09375
- w_expand: bfloat16 [512, 2048], P('rows'), may hold values from -0.25 to 0.25
- query_weight: bfloat16 [2048, 512], P('rows'), may hold values from -0.125 to 0.125
- w_key: bfloat16 [2048, 512], P('rows'), may hold values from -0.125 to 0.125
- w_value: bfloat16 [2048, 512], P('rows'), may hold values from -0.125 to 0.125
- w_out: bfloat16 [512, 2048], P('rows'), may hold values from -0.5 to 0.5
- w_head: bfloat16 [4096, 80], P('rows'), may hold values from -0.09375 to 0.09375
- gain_a: float32 [512], replicated, may hold values from 0.1 to 1.9
- bias_a: float32 [512], replicated, may hold values from -0.5 to 0.5
- gain_b: float32 [512], replicated, may hold values from 0.1 to 1.9
- bias_b: float32 [512], replicated, may hold values from -0.5 to 0.5
- gain_c: float32 [2048], replicated, may hold values from 0.1 to 1.9
- bias_c: float32 [2048], replicated, may hold values from -0.5 to 0.5
- ln_gain: float32 [512], replicated, may hold values from 0.1 to 1.9
- ln_bias: float32 [512], replicated, may hold values from -0.5 to 0.5
- head_bias: float32 [80], replicated, may hold values from -1 to 1
- bank: bfloat16 [320, 2048], P(('batch', 'rows')), may hold values from -6 to 6
- piece_box: int32 [256, 8], P(('batch', 'rows')), may hold values from 0 to 127
- piece_clip: int32 [256, 8], P(('batch', 'rows')), may hold values from 0 to 63
- send_count: int32 [256], P(('batch', 'rows')), may hold values from 0 to 8, as said below
- sample_pos: int32 [256, 224], P(('batch', 'rows')), may hold values from 0 to 15
- sample_weight: float32 [256, 224], P(('batch', 'rows')), may hold values from 0.01 to 0.06
- win_start: int32 [4096], P(('batch', 'rows')), may hold values from 0 to 60, as said below
- win_len: int32 [4096], P(('batch', 'rows')), may hold values from 20 to 40, as said below
- prob_cotangent: float32 [4096, 80], P(('batch', 'rows')), may hold values from -6 to 6
Outputs:
- probs: float32 [4096, 80], P(('batch', 'rows'))
- features_grad: bfloat16 [256, 8, 16, 2048], P('batch', 'rows')
- w_reduce_grad: float32 [2048, 512], P('rows', 'batch')
- w_spatial_grad: float32 [4608, 512], P('rows', 'batch')
- w_expand_grad: float32 [512, 2048], P('rows', 'batch')
- w_query_grad: float32 [2048, 512], P('rows', 'batch')
- w_key_grad: float32 [2048, 512], P('rows', 'batch')
- w_value_grad: float32 [2048, 512], P('rows', 'batch')
- w_out_grad: float32 [512, 2048], P('rows', 'batch')
- w_head_grad: float32 [4096, 80], P('rows', 'batch')
- gain_a_grad: float32 [512], replicated
- bias_a_grad: float32 [512], replicated
- gain_b_grad: float32 [512], replicated
- bias_b_grad: float32 [512], replicated
- gain_c_grad: float32 [2048], replicated
- bias_c_grad: float32 [2048], replicated
- ln_gain_grad: float32 [512], replicated
- ln_bias_grad: float32 [512], replicated
- classifier_bias_gradient: float32 [80], replicated
Inputs may be any that keep to these rules, and one draw needn't show every extreme that they name: `send_count`: at most 8 live slots from one device to one owner; some device sends exactly 8 to some owner in every draw. `win_len`: every window holds 20 to 40 entries, some box's exactly 40. win_start + win_len <= 80.
All inputs are finite; a program needn't handle non-finite values.
Results may differ from a plain program's by a relative error of at most 0.024.
Values may be sent and summed in bfloat16 or wider, within the bound.
A program may use at most 256 MiB of HBM per device.

v0:
```python
import jax
import jax.numpy as jnp
from jax import lax
from jax.sharding import PartitionSpec as P


def padded(cells, sides, width):
    for axis, dim in sides:
        count = lax.axis_size(axis)
        ends = count - 1
        head = lax.slice_in_dim(cells, 0, width, axis=dim)
        tail = lax.slice_in_dim(cells, cells.shape[dim] - width, cells.shape[dim], axis=dim)
        cells = jnp.concatenate(
            [
                lax.ppermute(tail, axis, [(i, (i + 1) % count) for i in range(ends)]),
                cells,
                lax.ppermute(head, axis, [((i + 1) % count, i) for i in range(ends)]),
            ],
            axis=dim,
        )
    return cells


def split_up(value, dim, peers):
    shape = value.shape
    parts = value.reshape(*shape[:dim], peers, shape[dim] // peers, *shape[dim + 1 :])
    return jnp.moveaxis(parts, dim, 0)


def sum_at_owner(value, axis, dim):
    peers = lax.axis_size(axis)
    parts = lax.all_to_all(split_up(value, dim, peers), axis, 0, 0, tiled=True)
    return jnp.sum(parts.astype(jnp.float32), axis=0)


def side_by_side(arrays, axis, dim, along):
    ends, at = ([], 0)
    for a in arrays[:-1]:
        at += a.shape[along]
        ends.append(at)
    both = jnp.concatenate(arrays, axis=along)
    return tuple(jnp.split(sum_at_owner(both, axis, dim), ends, axis=along))


def tdot(left, right):
    return lax.dot_general(
        left, right, (((0,), (0,)), ((), ())), preferred_element_type=jnp.float32
    )


def ndot(left, right):
    return lax.dot_general(
        left, right, (((1,), (1,)), ((), ())), preferred_element_type=jnp.float32
    )


def silu_slope(value):
    sig = jax.nn.sigmoid(value)
    return sig * (1.0 + value * (1.0 - sig))


def normalize(field, total_count):
    sums, squares = lax.psum((jnp.sum(field, 0), jnp.sum(field * field, 0)), ("batch", "rows"))
    centre_value = sums / total_count
    inverse = lax.rsqrt(squares / total_count - centre_value * centre_value + 1e-05)
    return ((field - centre_value) * inverse, inverse)


def segment_totals(grad, normed):
    return lax.psum((jnp.sum(grad, 0), jnp.sum(grad * normed, 0)), ("batch", "rows"))


def norm_back(grad, normed, inverse, gain, shift_sum, gain_total_grad, total_count):
    return (
        gain * inverse * (grad - shift_sum / total_count - normed * gain_total_grad / total_count)
    )


def on_device(
    features,
    w_reduce,
    w_spatial,
    w_expand,
    query_weight,
    w_key,
    w_value,
    w_out,
    w_head,
    gain_a,
    bias_a,
    gain_b,
    bias_b,
    gain_c,
    bias_c,
    ln_gain,
    ln_bias,
    head_bias,
    bank,
    piece_box,
    piece_clip,
    send_count,
    sample_pos,
    sample_weight,
    win_start,
    win_len,
    prob_cotangent,
):
    owners = lax.axis_size("rows")
    clip_dev, row_dev, col_count, d_in = features.shape
    cell_count = clip_dev * row_dev * col_count
    total_count = cell_count * owners * lax.axis_size("batch")
    w_a, w_b, w_c, w_q, w_k, w_v, w_o, w_h = (
        lax.all_gather(w_reduce, "rows", axis=0, tiled=True),
        lax.all_gather(w_spatial, "rows", axis=0, tiled=True),
        lax.all_gather(w_expand, "rows", axis=0, tiled=True),
        lax.all_gather(query_weight, "rows", axis=0, tiled=True),
        lax.all_gather(w_key, "rows", axis=0, tiled=True),
        lax.all_gather(w_value, "rows", axis=0, tiled=True),
        lax.all_gather(w_out, "rows", axis=0, tiled=True),
        lax.all_gather(w_head, "rows", axis=0, tiled=True),
    )
    d_mid = w_a.shape[1]
    flat_x = features.reshape(cell_count, d_in)
    pre_a = jnp.dot(flat_x, w_a, preferred_element_type=jnp.float32)
    hat_a, inverse_a = normalize(pre_a, total_count)
    act_a = gain_a * hat_a + bias_a
    low_a = jax.nn.silu(act_a).astype(jnp.bfloat16)
    halo_a = padded(low_a.reshape(clip_dev, row_dev, col_count, d_mid), (("rows", 1),), 1)
    halo_a = jnp.pad(halo_a, ((0, 0), (0, 0), (1, 1), (0, 0)))
    window_a = jnp.concatenate(
        [
            halo_a[:, row_step : row_step + row_dev, col_step : col_step + col_count]
            for row_step in range(3)
            for col_step in range(3)
        ],
        axis=3,
    ).reshape(cell_count, 9 * d_mid)
    pre_b = jnp.dot(window_a, w_b, preferred_element_type=jnp.float32)
    hat_b, inverse_b = normalize(pre_b, total_count)
    act_b = gain_b * hat_b + bias_b
    low_b = jax.nn.silu(act_b).astype(jnp.bfloat16)
    pre_c = jnp.dot(low_b, w_c, preferred_element_type=jnp.float32)
    hat_c, inverse_c = normalize(pre_c, total_count)
    pre_out = gain_c * hat_c + bias_c + flat_x.astype(jnp.float32)
    fmap = jax.nn.silu(pre_out).astype(jnp.bfloat16)
    capacity = piece_box.shape[1]
    samples = sample_pos.shape[1] // capacity
    slot_count = owners * capacity
    sample_cells = (
        piece_clip[:, :, None] * (row_dev * col_count)
        + sample_pos.reshape(owners, capacity, samples)
    ).reshape(slot_count, samples)
    is_live = (jnp.arange(capacity)[None, :] < send_count[:, None]).reshape(slot_count)
    slot_weights = sample_weight.reshape(slot_count, samples) * is_live[:, None].astype(jnp.float32)
    cell_ids = jnp.arange(cell_count)[None, :]
    interp_sum = jnp.zeros((slot_count, cell_count), jnp.float32)
    for sample_index in range(samples):
        interp_sum = interp_sum + jnp.where(
            sample_cells[:, sample_index, None] == cell_ids,
            slot_weights[:, sample_index, None],
            0.0,
        )
    interpolated_value = interp_sum.astype(jnp.bfloat16)
    region_parts = (
        jnp.dot(interpolated_value, fmap, preferred_element_type=jnp.float32)
        .astype(jnp.bfloat16)
        .reshape(owners, capacity, d_in)
    )
    arrived, arrived_box = (
        lax.all_to_all(region_parts, "rows", split_axis=0, concat_axis=0, tiled=True),
        lax.all_to_all(piece_box, "rows", split_axis=0, concat_axis=0, tiled=True),
    )
    box_dev = win_start.shape[0]
    flat_box = arrived_box.reshape(slot_count)
    owner_hits = (flat_box[None, :] == jnp.arange(box_dev)[:, None]).astype(jnp.bfloat16)
    pooled = jnp.dot(
        owner_hits, arrived.reshape(slot_count, d_in), preferred_element_type=jnp.float32
    )
    pooled_low = pooled.astype(jnp.bfloat16)
    keys_own = jnp.dot(bank, w_k, preferred_element_type=jnp.float32).astype(jnp.bfloat16)
    values_own = jnp.dot(bank, w_v, preferred_element_type=jnp.float32).astype(jnp.bfloat16)
    key_rows, value_rows = (
        lax.all_gather(keys_own, "rows", axis=0, tiled=True),
        lax.all_gather(values_own, "rows", axis=0, tiled=True),
    )
    bank_length = key_rows.shape[0]
    queries = jnp.dot(pooled_low, w_q, preferred_element_type=jnp.float32).astype(jnp.bfloat16)
    score_scale = d_mid ** (-0.5)
    scores = ndot(queries, key_rows) * score_scale
    positions = jnp.arange(bank_length)[None, :]
    window_mask = (positions >= win_start[:, None]) & (positions < (win_start + win_len)[:, None])
    attend = jax.nn.softmax(jnp.where(window_mask, scores, -1e30), axis=-1)
    attend_low = attend.astype(jnp.bfloat16)
    mixture = jnp.dot(attend_low, value_rows, preferred_element_type=jnp.float32)
    centred = mixture - jnp.mean(mixture, axis=-1, keepdims=True)
    inverse_z = lax.rsqrt(jnp.mean(centred * centred, axis=-1, keepdims=True) + 1e-05)
    hat_z = centred * inverse_z
    pre_ln = ln_gain * hat_z + ln_bias
    low_r = jax.nn.silu(pre_ln).astype(jnp.bfloat16)
    branch = jnp.dot(low_r, w_o, preferred_element_type=jnp.float32)
    joined = jnp.concatenate([pooled, pooled + branch], axis=1).astype(jnp.bfloat16)
    logits = jnp.dot(joined, w_h, preferred_element_type=jnp.float32) + head_bias
    likely = jax.nn.sigmoid(logits)
    d_logit = (prob_cotangent * (likely * (1.0 - likely))).astype(jnp.bfloat16)
    grad_head_bias = jnp.sum(d_logit.astype(jnp.float32), 0)
    grad_wh = tdot(joined, d_logit)
    d_joined = ndot(d_logit, w_h)
    d_pooled = d_joined[:, :d_in] + d_joined[:, d_in:]
    d_branch = d_joined[:, d_in:].astype(jnp.bfloat16)
    grad_wo = tdot(low_r, d_branch)
    d_ln = ndot(d_branch, w_o) * silu_slope(pre_ln)
    grad_ln_gain = jnp.sum(d_ln * hat_z, 0)
    grad_ln_bias = jnp.sum(d_ln, 0)
    d_hat = d_ln * ln_gain
    d_mixture = (
        inverse_z
        * (
            d_hat
            - jnp.mean(d_hat, axis=-1, keepdims=True)
            - hat_z * jnp.mean(d_hat * hat_z, axis=-1, keepdims=True)
        )
    ).astype(jnp.bfloat16)
    d_attend = ndot(d_mixture, value_rows)
    d_values = tdot(attend_low, d_mixture)
    d_scores = (attend * (d_attend - jnp.sum(d_attend * attend, axis=-1, keepdims=True))).astype(
        jnp.bfloat16
    )
    d_queries = (
        jnp.dot(d_scores, key_rows, preferred_element_type=jnp.float32) * score_scale
    ).astype(jnp.bfloat16)
    d_keys = tdot(d_scores, queries) * score_scale
    grad_wq = tdot(pooled_low, d_queries)
    d_pooled = d_pooled + ndot(d_queries, w_q)
    key_sum, value_sum = side_by_side(
        (d_keys.astype(jnp.bfloat16), d_values.astype(jnp.bfloat16)), "rows", 0, 1
    )
    grad_wk = tdot(bank, key_sum.astype(jnp.bfloat16))
    grad_wv = tdot(bank, value_sum.astype(jnp.bfloat16))
    back_pieces = jnp.take(d_pooled.astype(jnp.bfloat16), flat_box, axis=0).reshape(
        owners, capacity, d_in
    )
    returned = lax.all_to_all(back_pieces, "rows", split_axis=0, concat_axis=0, tiled=True)
    d_fmap = tdot(interpolated_value, returned.reshape(slot_count, d_in))
    d_pre = d_fmap * silu_slope(pre_out)
    head_sums = lax.psum(
        (jnp.sum(d_pre, 0), jnp.sum(d_pre * hat_c, 0), grad_ln_gain, grad_ln_bias, grad_head_bias),
        ("batch", "rows"),
    )
    d_c = norm_back(
        d_pre, hat_c, inverse_c, gain_c, head_sums[0], head_sums[1], total_count
    ).astype(jnp.bfloat16)
    grad_wc = tdot(low_b, d_c)
    d_act_b = ndot(d_c, w_c) * silu_slope(act_b)
    shift_b_sum, gain_b_sum = segment_totals(d_act_b, hat_b)
    d_b = norm_back(d_act_b, hat_b, inverse_b, gain_b, shift_b_sum, gain_b_sum, total_count).astype(
        jnp.bfloat16
    )
    grad_wb = tdot(window_a, d_b)
    halo_d = padded(d_b.reshape(clip_dev, row_dev, col_count, d_mid), (("rows", 1),), 1)
    halo_d = jnp.pad(halo_d, ((0, 0), (0, 0), (1, 1), (0, 0)))
    window_d = jnp.concatenate(
        [
            halo_d[
                :, 2 - row_step : 2 - row_step + row_dev, 2 - col_step : 2 - col_step + col_count
            ]
            for row_step in range(3)
            for col_step in range(3)
        ],
        axis=3,
    ).reshape(cell_count, 9 * d_mid)
    flipped = w_b.reshape(9, d_mid, d_mid).transpose(0, 2, 1).reshape(9 * d_mid, d_mid)
    d_act_a = jnp.dot(window_d, flipped, preferred_element_type=jnp.float32) * silu_slope(act_a)
    shift_a_sum, gain_a_sum = segment_totals(d_act_a, hat_a)
    d_a = norm_back(d_act_a, hat_a, inverse_a, gain_a, shift_a_sum, gain_a_sum, total_count).astype(
        jnp.bfloat16
    )
    grad_wa = tdot(flat_x, d_a)
    grad_input = (ndot(d_a, w_a) + d_pre).astype(jnp.bfloat16).reshape(features.shape)
    partial_sums = (
        lax.psum_scatter(grad_wa, "rows", scatter_dimension=0, tiled=True),
        lax.psum_scatter(grad_wb, "rows", scatter_dimension=0, tiled=True),
        lax.psum_scatter(grad_wc, "rows", scatter_dimension=0, tiled=True),
        lax.psum_scatter(grad_wq, "rows", scatter_dimension=0, tiled=True),
        lax.psum_scatter(grad_wk, "rows", scatter_dimension=0, tiled=True),
        lax.psum_scatter(grad_wv, "rows", scatter_dimension=0, tiled=True),
        lax.psum_scatter(grad_wo, "rows", scatter_dimension=0, tiled=True),
        lax.psum_scatter(grad_wh, "rows", scatter_dimension=0, tiled=True),
    )
    finished = (
        lax.psum_scatter(
            partial_sums[0].astype(jnp.bfloat16), "batch", scatter_dimension=1, tiled=True
        ).astype(jnp.float32),
        lax.psum_scatter(
            partial_sums[1].astype(jnp.bfloat16), "batch", scatter_dimension=1, tiled=True
        ).astype(jnp.float32),
        lax.psum_scatter(
            partial_sums[2].astype(jnp.bfloat16), "batch", scatter_dimension=1, tiled=True
        ).astype(jnp.float32),
        lax.psum_scatter(
            partial_sums[3].astype(jnp.bfloat16), "batch", scatter_dimension=1, tiled=True
        ).astype(jnp.float32),
        lax.psum_scatter(
            partial_sums[4].astype(jnp.bfloat16), "batch", scatter_dimension=1, tiled=True
        ).astype(jnp.float32),
        lax.psum_scatter(
            partial_sums[5].astype(jnp.bfloat16), "batch", scatter_dimension=1, tiled=True
        ).astype(jnp.float32),
        lax.psum_scatter(
            partial_sums[6].astype(jnp.bfloat16), "batch", scatter_dimension=1, tiled=True
        ).astype(jnp.float32),
        lax.psum_scatter(
            partial_sums[7].astype(jnp.bfloat16), "batch", scatter_dimension=1, tiled=True
        ).astype(jnp.float32),
    )
    return (
        likely,
        grad_input,
        finished[0],
        finished[1],
        finished[2],
        finished[3],
        finished[4],
        finished[5],
        finished[6],
        finished[7],
        gain_a_sum,
        shift_a_sum,
        gain_b_sum,
        shift_b_sum,
        head_sums[1],
        head_sums[0],
        head_sums[2],
        head_sums[3],
        head_sums[4],
    )


def solution(mesh):
    return jax.shard_map(
        on_device,
        mesh=mesh,
        in_specs=(
            P("batch", "rows", None, None),
            P("rows", None),
            P("rows", None),
            P("rows", None),
            P("rows", None),
            P("rows", None),
            P("rows", None),
            P("rows", None),
            P("rows", None),
            P(),
            P(),
            P(),
            P(),
            P(),
            P(),
            P(),
            P(),
            P(),
            P(("batch", "rows"), None),
            P(("batch", "rows"), None),
            P(("batch", "rows"), None),
            P(("batch", "rows")),
            P(("batch", "rows"), None),
            P(("batch", "rows"), None),
            P(("batch", "rows")),
            P(("batch", "rows")),
            P(("batch", "rows"), None),
        ),
        out_specs=(
            P(("batch", "rows"), None),
            P("batch", "rows", None, None),
            P("rows", "batch"),
            P("rows", "batch"),
            P("rows", "batch"),
            P("rows", "batch"),
            P("rows", "batch"),
            P("rows", "batch"),
            P("rows", "batch"),
            P("rows", "batch"),
            P(),
            P(),
            P(),
            P(),
            P(),
            P(),
            P(),
            P(),
            P(),
        ),
        check_vma=False,
    )
```

profile of v0, /device:TPU:0, one launch (start us, length us, event | category | flops | bytes accessed | tf_op | source)
XLA Modules:
  0.0 1011.4 jit_solution(11663919438469440399)
XLA Ops:
  11.2 6.3 all-to-all-start
  19.9 21.7 %all-gather.10.cloned.1.call-done = bf16[2048,512]{1,0:T(8,128)(2,1)} async-done(((bf16[256,512]{1,0:T(8,128)(2,1)}), bf16[2048,512]{1,0:T(8,128)(2,1)}) %all-gather.10.cloned.1.call-update) | async-done | bytes 2097168 | tf_op jit(solution)/shard_map/all_gather | solution.py:113
  41.6 5.2 fusion.49
  46.9 42.2 %all-reduce.8 = (f32[512]{0:T(512)S(1)}, f32[512]{0:T(512)S(1)}) all-reduce(f32[512]{0:T(512)S(1)} %get-tuple-element.106, f32[512]{0:T(512)S(1)} %get-tuple-element.105), channel_id=1, replica_groups=mesh['batch'=4,'rows'=8] {'batch','rows'}, use_global_device_ids=true, to_apply=%region_3.0 | all-reduce | flops 1024 | bytes 8192 | tf_op jit(solution)/shard_map/psum | solution.py:63
  97.0 39.7 %all_gather.39 = bf16[4096,80]{0,1:T(8,128)(2,1)} all-gather(bf16[512,80]{0,1:T(8,128)(2,1)S(1)} %copy-done.8), channel_id=1, replica_groups=mesh['batch'=4,'rows'=8] {'rows'}, dimensions={0}, use_global_device_ids=true | all-gather | bytes 737280 | tf_op jit(solution)/shard_map/all_gather | solution.py:120
  138.5 3.6 select_maximum_fusion.2
  157.1 10.1 %fusion.48 = (f32[512]{0:T(512)S(1)}, f32[512]{0:T(512)S(1)}, f32[1024,512]{1,0:T(8,128)}) fusion(bf16[1024,4608]{1,0:T(8,128)(2,1)} %constant_dynamic-update-slice_fusion, bf16[4608,512]{1,0:T(8,128)(2,1)} %all-gather.12.cloned.1.call-done), kind=kOutput, calls=%fused_computation.239 | convolution fusion | flops 4833410048 | bytes 16257024 | tf_op jit(solution)/shard_map/dot_general | solution.py:138
  167.2 41.5 %all-reduce.7 = (f32[512]{0:T(512)S(1)}, f32[512]{0:T(512)S(1)}) all-reduce(f32[512]{0:T(512)S(1)} %get-tuple-element.104, f32[512]{0:T(512)S(1)} %get-tuple-element.103), channel_id=1, replica_groups=mesh['batch'=4,'rows'=8] {'batch','rows'}, use_global_device_ids=true, to_apply=%region_7.8 | all-reduce | flops 1024 | bytes 8192 | tf_op jit(solution)/shard_map/psum | solution.py:63
  208.9 8.2 fusion.45
  217.0 42.3 %all-reduce.6 = (f32[2048]{0:T(1024)S(1)}, f32[2048]{0:T(1024)S(1)}) all-reduce(f32[2048]{0:T(1024)S(1)} %get-tuple-element.98, f32[2048]{0:T(1024)S(1)} %get-tuple-element.97), channel_id=1, replica_groups=mesh['batch'=4,'rows'=8] {'batch','rows'}, use_global_device_ids=true, to_apply=%region_11.12 | all-reduce | flops 4096 | bytes 32768 | tf_op jit(solution)/shard_map/psum | solution.py:63
  259.8 10.3 %fusion.6 = bf16[8,8,2048]{2,1,0:T(8,128)(2,1)} fusion(bf16[1024,2048]{1,0:T(8,128)(2,1)} %bitcast.110, f32[2048]{0:T(1024)S(1)} %copy-done.116, f32[2048]{0:T(1024)S(1)} %get-tuple-element.197, f32[1024,2048]{1,0:T(8,128)} %get-tuple-element.207, f32[2048]{0:T(1024)S(1)} %get-tuple-element.198, f32[2048]{0:T(1024)S(1)} %copy-done.20, ...), kind=kOutput, calls=%fused_computation.27 | convolution fusion | flops 297140224 | bytes 12892160 | tf_op jit(solution)/shard_map/dot_general | solution.py:165
  270.1 3.4 all-to-all-start.1
  275.5 15.3 %all-gather = bf16[8,10,512]{2,1,0:T(8,128)(2,1)S(1)} all-gather(bf16[1,10,512]{2,1,0:T(8,128)(2,1)S(1)} %fusion.14), channel_id=1, replica_groups=mesh['batch'=4,'rows'=8] {'rows'}, dimensions={0}, use_global_device_ids=true | all-gather | bytes 92160 | tf_op jit(solution)/shard_map/all_gather | solution.py:183
  292.9 14.4 %all-gather.1 = bf16[8,10,512]{2,1,0:T(8,128)(2,1)S(1)} all-gather(bf16[1,10,512]{2,1,0:T(8,128)(2,1)S(1)} %fusion.15), channel_id=1, replica_groups=mesh['batch'=4,'rows'=8] {'rows'}, dimensions={0}, use_global_device_ids=true | all-gather | bytes 92160 | tf_op jit(solution)/shard_map/all_gather | solution.py:184
  313.9 2.8 convert_reduce_fusion
  321.0 3.1 multiply_reduce_fusion.6
  324.8 2.7 fusion.58
  327.6 4.1 fusion.20
  332.2 16.3 %all_to_all.24 = bf16[8,10,1024]{2,1,0:T(8,128)(2,1)S(1)} all-to-all(bf16[8,10,1024]{2,1,0:T(8,128)(2,1)S(1)} %reshape.231), channel_id=1, replica_groups=mesh['batch'=4,'rows'=8] {'rows'}, dimensions={0} | all-to-all | bytes 327680 | tf_op jit(solution)/shard_map/all_to_all | solution.py:32
  348.6 2.7 convolution_bitcast_fusion.1
  354.7 3.0 fusion.4
  358.5 17.0 %all_to_all.25 = bf16[8,8,2048]{2,1,0:T(8,128)(2,1)S(1)} all-to-all(bf16[8,8,2048]{2,1,0:T(8,128)(2,1)S(1)} %bitcast_select_fusion), channel_id=1, replica_groups=mesh['batch'=4,'rows'=8] {'rows'}, dimensions={0} | all-to-all | bytes 524288 | tf_op jit(solution)/shard_map/all_to_all | solution.py:242
  375.9 14.8 %fusion.44 = (f32[2048]{0:T(1024)S(1)}, f32[2048]{0:T(1024)S(1)}, f32[1024,2048]{1,0:T(8,128)}) fusion(f32[2048]{0:T(1024)S(1)} %get-tuple-element.197, f32[1024,2048]{1,0:T(8,128)} %get-tuple-element.207, f32[2048]{0:T(1024)S(1)} %get-tuple-element.198, bf16[1024,2048]{1,0:T(8,128)(2,1)} %bitcast.111, f32[2048]{0:T(1024)} %param.41, ...), kind=kOutput, calls=%fused_computation.235 | convolution fusion | flops 309587968 | bytes 21297152 | tf_op jit(solution)/shard_map/dot_general | solution.py:46
  390.7 38.9 %all-reduce.5 = (f32[2048]{0:T(1024)S(1)}, f32[2048]{0:T(1024)S(1)}) all-reduce(f32[2048]{0:T(1024)S(1)} %get-tuple-element.96, f32[2048]{0:T(1024)S(1)} %get-tuple-element.95), channel_id=1, replica_groups=mesh['batch'=4,'rows'=8] {'batch','rows'}, use_global_device_ids=true, to_apply=%region_22.23 | all-reduce | flops 4096 | bytes 32768 | tf_op jit(solution)/shard_map/psum | solution.py:245
  429.7 7.4 multiply_convert_fusion
  439.2 4.6 fusion.42
  444.0 8.1 fusion.47
  452.1 42.8 %all-reduce.4 = (f32[512]{0:T(512)S(1)}, f32[512]{0:T(512)S(1)}) all-reduce(f32[512]{0:T(512)S(1)} %get-tuple-element.102, f32[512]{0:T(512)S(1)} %get-tuple-element.101), channel_id=1, replica_groups=mesh['batch'=4,'rows'=8] {'batch','rows'}, use_global_device_ids=true, to_apply=%region_26.27 | all-reduce | flops 1024 | bytes 8192 | tf_op jit(solution)/shard_map/psum | solution.py:70
  494.8 2.9 multiply_convert_fusion.8
  497.7 2.7 collective-permute-start.2
  501.7 6.7 copy.62
  508.4 3.6 select_maximum_fusion
  518.0 7.1 fusion.46
  525.2 53.3 %all-reduce.3 = (f32[512]{0:T(512)S(1)}, f32[512]{0:T(512)S(1)}, f32[512]{0:T(512)}, f32[512]{0:T(512)}, f32[80]{0:T(128)}) all-reduce(f32[512]{0:T(512)S(1)} %get-tuple-element.100, f32[512]{0:T(512)S(1)} %get-tuple-element.99, f32[512]{0:T(512)S(1)} %copy-done.28, ...), channel_id=1, replica_groups=mesh['batch'=4,'rows'=8] {'batch','rows'}, use_global_device_ids=true, to_apply=%region_30.31 | all-reduce | flops 2128 | bytes 17024 | tf_op jit(solution)/shard_map/psum | solution.py:70
  581.8 4.4 convolution_bitcast_fusion.2
  586.3 11.4 %fusion.57 = f32[4608,512]{1,0:T(8,128)} fusion(bf16[1024,4608]{1,0:T(8,128)(2,1)} %constant_dynamic-update-slice_fusion, bf16[1024,512]{1,0:T(8,128)(2,1)S(1)} %multiply_convert_fusion.8), kind=kOutput, calls=%fused_computation.247 | convolution fusion | flops 4831838208 | bytes 19922944 | tf_op jit(solution)/shard_map/dot_general | solution.py:46
  607.2 10.4 %reduce-scatter.26.cloned.1.call-done = f32[64,2048]{1,0:T(8,128)} async-done(((f32[512,2048]{1,0:T(8,128)}), f32[64,2048]{1,0:T(8,128)}) %reduce-scatter.26.cloned.1.call-update) | async-done | bytes 524304 | tf_op jit(solution)/shard_map/reduce_scatter | solution.py:282
  619.5 49.1 %reduce-scatter.20.cloned.1.call-done = f32[256,512]{0,1:T(8,128)} async-done(((f32[2048,512]{0,1:T(8,128)}), f32[256,512]{0,1:T(8,128)}) %reduce-scatter.20.cloned.1.call-update) | async-done | bytes 524304 | tf_op jit(solution)/shard_map/reduce_scatter | solution.py:280
  670.4 98.0 %reduce-scatter.24.cloned.1.call-done = f32[576,512]{1,0:T(8,128)} async-done(((f32[4608,512]{1,0:T(8,128)}), f32[576,512]{1,0:T(8,128)}) %reduce-scatter.24.cloned.1.call-update) | async-done | bytes 1179664 | tf_op jit(solution)/shard_map/reduce_scatter | solution.py:281
  772.2 8.5 add_convert_fusion
  780.7 30.6 %all-reduce.11.cloned.1.call-done = bf16[512,80]{0,1:T(8,128)(2,1)} async-done(((bf16[512,80]{0,1:T(8,128)(2,1)}), bf16[512,80]{0,1:T(8,128)(2,1)}) %all-reduce.11.cloned.1.call-update) | async-done | bytes 81936
  812.6 26.3 %reduce-scatter.48.cloned.1.call-done = bf16[128,256]{1,0:T(8,128)(2,1)} async-done(((bf16[512,256]{1,0:T(8,128)(2,1)}), bf16[128,256]{1,0:T(8,128)(2,1)}) %reduce-scatter.48.cloned.1.call-update) | async-done | bytes 65552
  840.5 25.1 %reduce-scatter.42.cloned.1.call-done = bf16[64,512]{1,0:T(8,128)(2,1)} async-done(((bf16[64,2048]{1,0:T(8,128)(2,1)}), bf16[64,512]{1,0:T(8,128)(2,1)}) %reduce-scatter.42.cloned.1.call-update) | async-done | bytes 65552 | tf_op jit(solution)/shard_map/reduce_scatter | solution.py:308
  867.2 25.6 %reduce-scatter.34.cloned.1.call-done = bf16[256,128]{0,1:T(8,128)(2,1)} async-done(((bf16[256,512]{0,1:T(8,128)(2,1)}), bf16[256,128]{0,1:T(8,128)(2,1)}) %reduce-scatter.34.cloned.1.call-update) | async-done | bytes 65552 | tf_op jit(solution)/shard_map/reduce_scatter | solution.py:302
  894.4 25.1 %reduce-scatter.38.cloned.1.call-done = bf16[256,128]{0,1:T(8,128)(2,1)} async-done(((bf16[256,512]{0,1:T(8,128)(2,1)}), bf16[256,128]{0,1:T(8,128)(2,1)}) %reduce-scatter.38.cloned.1.call-update) | async-done | bytes 65552 | tf_op jit(solution)/shard_map/reduce_scatter | solution.py:305
  921.1 25.5 %reduce-scatter.28.cloned.1.call-done = bf16[64,512]{1,0:T(8,128)(2,1)} async-done(((bf16[64,2048]{1,0:T(8,128)(2,1)}), bf16[64,512]{1,0:T(8,128)(2,1)}) %reduce-scatter.28.cloned.1.call-update) | async-done | bytes 65552 | tf_op jit(solution)/shard_map/reduce_scatter | solution.py:296
  948.1 26.0 %reduce-scatter.22.cloned.1.call-done = bf16[256,128]{0,1:T(8,128)(2,1)} async-done(((bf16[256,512]{0,1:T(8,128)(2,1)}), bf16[256,128]{0,1:T(8,128)(2,1)}) %reduce-scatter.22.cloned.1.call-update) | async-done | bytes 65552 | tf_op jit(solution)/shard_map/reduce_scatter | solution.py:290
  975.6 27.0 %reduce-scatter.46.cloned.1.call-done = bf16[128,576]{1,0:T(8,128)(2,1)} async-done(((bf16[512,576]{1,0:T(8,128)(2,1)}), bf16[128,576]{1,0:T(8,128)(2,1)}) %reduce-scatter.46.cloned.1.call-update) | async-done | bytes 147472
  (412 shorter events, 92.2 us)
Async XLA Ops:
  7.2 266.4 %copy-start = (bf16[10,2048]{1,0:T(8,128)(2,1)S(1)}, bf16[10,2048]{1,0:T(8,128)(2,1)}, u32[]{:S(2)}) copy-start(bf16[10,2048]{1,0:T(8,128)(2,1)} %param.45) | copy-start | bytes 122884
  7.2 34.4 %all-gather.10.cloned.1.call-start = ((), (), s32[]{:S(2)}) async-start(), calls=%async_computation.19 | async-start | bytes 2359296 | tf_op jit(solution)/shard_map/all_gather | solution.py:113
  7.9 149.2 %all-gather.12.cloned.1.call-start = ((), (), s32[]{:S(2)}) async-start(), calls=%async_computation.20 | async-start | bytes 5308416 | tf_op jit(solution)/shard_map/all_gather | solution.py:114
  8.7 200.1 %all-gather.14.cloned.1.call-start = ((), (), s32[]{:S(2)}) async-start(), calls=%async_computation.21 | async-start | bytes 2359296 | tf_op jit(solution)/shard_map/all_gather | solution.py:115
  9.4 264.1 %all-gather.18.cloned.1.call-start = ((), (), s32[]{:S(2)}) async-start(), calls=%async_computation.23 | async-start | bytes 2359296 | tf_op jit(solution)/shard_map/all_gather | solution.py:117
  10.0 280.9 %all-gather.20.cloned.1.call-start = ((), (), s32[]{:S(2)}) async-start(), calls=%async_computation.24 | async-start | bytes 2359296 | tf_op jit(solution)/shard_map/all_gather | solution.py:118
  10.6 298.0 %all-gather.16.cloned.1.call-start = ((), (), s32[]{:S(2)}) async-start(), calls=%async_computation.22 | async-start | bytes 2359296 | tf_op jit(solution)/shard_map/all_gather | solution.py:116
  11.2 126.1 %all-to-all-start = ((s32[8,1,8]{2,1,0:T(1,128)}), s32[8,1,8]{2,1,0:T(1,128)S(1)}, u32[]{:S(2)}, u32[]{:S(2)}) async-start(s32[8,1,8]{2,1,0:T(1,128)} %bitcast.138), calls=%async_computation | async-start | bytes 8192 | tf_op jit(solution)/shard_map/all_to_all | solution.py:171
  17.5 293.9 %all-gather.22.cloned.1.call-start = ((), (), s32[]{:S(2)}) async-start(), calls=%async_computation.25 | async-start | bytes 2359296 | tf_op jit(solution)/shard_map/all_gather | solution.py:119
  89.8 48.7 %collective-permute-start = (bf16[64,1,16,512]{3,2,0,1:T(8,128)(2,1)S(1)}, bf16[64,1,16,512]{3,2,0,1:T(8,128)(2,1)}, u32[]{:S(2)}, u32[]{:S(2)}) collective-permute-start(bf16[64,1,16,512]{3,2,0,1:T(8,128)(2,1)S(1)} %bitcast.117), channel_id=1, source_target_pairs={{0,1},{1,2},{2,3},{3,4},{4,5},{5,6},{6,7},{8,9},{9,10},{10,11},{11... | collective-permute-start | bytes 3145736 | tf_op jit(solution)/shard_map/ppermute | solution.py:15
  92.5 46.0 %collective-permute-start.1 = (bf16[64,1,16,512]{3,2,0,1:T(8,128)(2,1)S(1)}, bf16[64,1,16,512]{3,2,0,1:T(8,128)(2,1)}, u32[]{:S(2)}, u32[]{:S(2)}) collective-permute-start(bf16[64,1,16,512]{3,2,0,1:T(8,128)(2,1)S(1)} %bitcast.118), channel_id=1, source_target_pairs={{1,0},{2,1},{3,2},{4,3},{5,4},{6,5},{7,6},{9,8},{10,9},{11,10},{12... | collective-permute-start | bytes 3145736 | tf_op jit(solution)/shard_map/ppermute | solution.py:17
  94.4 165.0 %copy-start.35 = (s32[64]{0:T(128)}, s32[64]{0:T(128)S(1)}, u32[]{:S(2)}) copy-start(s32[64]{0:T(128)S(1)} %get-tuple-element.149) | copy-start | bytes 772
  94.4 165.0 %copy-start.37 = (s32[64]{0:T(128)}, s32[64]{0:T(128)S(1)}, u32[]{:S(2)}) copy-start(s32[64]{0:T(128)S(1)} %get-tuple-element.150) | copy-start | bytes 772
  94.4 165.0 %copy-start.39 = (s32[64]{0:T(128)}, s32[64]{0:T(128)S(1)}, u32[]{:S(2)}) copy-start(s32[64]{0:T(128)S(1)} %get-tuple-element.151) | copy-start | bytes 772
  94.4 165.0 %copy-start.41 = (s32[64]{0:T(128)}, s32[64]{0:T(128)S(1)}, u32[]{:S(2)}) copy-start(s32[64]{0:T(128)S(1)} %get-tuple-element.152) | copy-start | bytes 772
  94.4 165.0 %copy-start.43 = (s32[64]{0:T(128)}, s32[64]{0:T(128)S(1)}, u32[]{:S(2)}) copy-start(s32[64]{0:T(128)S(1)} %get-tuple-element.153) | copy-start | bytes 772
  94.5 165.0 %copy-start.45 = (s32[64]{0:T(128)}, s32[64]{0:T(128)S(1)}, u32[]{:S(2)}) copy-start(s32[64]{0:T(128)S(1)} %get-tuple-element.154) | copy-start | bytes 772
  94.5 165.0 %copy-start.47 = (s32[64]{0:T(128)}, s32[64]{0:T(128)S(1)}, u32[]{:S(2)}) copy-start(s32[64]{0:T(128)S(1)} %get-tuple-element.155) | copy-start | bytes 772
  94.5 165.0 %copy-start.49 = (s32[64]{0:T(128)}, s32[64]{0:T(128)S(1)}, u32[]{:S(2)}) copy-start(s32[64]{0:T(128)S(1)} %get-tuple-element.156) | copy-start | bytes 772
  94.5 165.0 %copy-start.51 = (s32[64]{0:T(128)}, s32[64]{0:T(128)S(1)}, u32[]{:S(2)}) copy-start(s32[64]{0:T(128)S(1)} %get-tuple-element.157) | copy-start | bytes 772
  95.7 163.9 %copy-start.83 = (s32[64]{0:T(128)}, s32[64]{0:T(128)S(1)}, u32[]{:S(2)}) copy-start(s32[64]{0:T(128)S(1)} %get-tuple-element.116) | copy-start | bytes 772
  95.7 163.9 %copy-start.85 = (s32[64]{0:T(128)}, s32[64]{0:T(128)S(1)}, u32[]{:S(2)}) copy-start(s32[64]{0:T(128)S(1)} %get-tuple-element.117) | copy-start | bytes 772
  95.7 163.9 %copy-start.87 = (s32[64]{0:T(128)}, s32[64]{0:T(128)S(1)}, u32[]{:S(2)}) copy-start(s32[64]{0:T(128)S(1)} %get-tuple-element.118) | copy-start | bytes 772
  95.7 163.9 %copy-start.89 = (s32[64]{0:T(128)}, s32[64]{0:T(128)S(1)}, u32[]{:S(2)}) copy-start(s32[64]{0:T(128)S(1)} %get-tuple-element.119) | copy-start | bytes 772
  95.7 163.9 %copy-start.91 = (s32[64]{0:T(128)}, s32[64]{0:T(128)S(1)}, u32[]{:S(2)}) copy-start(s32[64]{0:T(128)S(1)} %get-tuple-element.120) | copy-start | bytes 772
  95.7 163.9 %copy-start.93 = (s32[64]{0:T(128)}, s32[64]{0:T(128)S(1)}, u32[]{:S(2)}) copy-start(s32[64]{0:T(128)S(1)} %get-tuple-element.121) | copy-start | bytes 772
  270.1 37.2 %all-to-all-start.1 = ((bf16[8,8,2048]{2,1,0:T(8,128)(2,1)}), bf16[8,8,2048]{2,1,0:T(8,128)(2,1)S(1)}, u32[]{:S(2)}, u32[]{:S(2)}) async-start(bf16[8,8,2048]{2,1,0:T(8,128)(2,1)} %fusion.6), calls=%async_computation.1 | async-start | bytes 524288 | tf_op jit(solution)/shard_map/all_to_all | solution.py:170
  273.5 324.3 %reduce-scatter.44.cloned.1.call-start = ((), (), s32[]{:S(2)}) async-start(), calls=%async_computation.38 | async-start | bytes 1474560 | tf_op jit(solution)/shard_map/reduce_scatter | solution.py:287
  318.1 281.4 %reduce-scatter.30.cloned.1.call-start = ((), (), s32[]{:S(2)}) async-start(), calls=%async_computation.31 | async-start | bytes 4718592 | tf_op jit(solution)/shard_map/reduce_scatter | solution.py:283
  327.5 274.0 %reduce-scatter.40.cloned.1.call-start = ((), (), s32[]{:S(2)}) async-start(), calls=%async_computation.36 | async-start | bytes 4718592 | tf_op jit(solution)/shard_map/reduce_scatter | solution.py:286
  331.8 271.6 %reduce-scatter.32.cloned.1.call-start = ((), (), s32[]{:S(2)}) async-start(), calls=%async_computation.32 | async-start | bytes 4718592 | tf_op jit(solution)/shard_map/reduce_scatter | solution.py:284
  351.4 254.0 %reduce-scatter.36.cloned.1.call-start = ((), (), s32[]{:S(2)}) async-start(), calls=%async_computation.34 | async-start | bytes 4718592 | tf_op jit(solution)/shard_map/reduce_scatter | solution.py:285
  354.5 263.1 %reduce-scatter.26.cloned.1.call-start = ((), (), s32[]{:S(2)}) async-start(), calls=%async_computation.29 | async-start | bytes 4718592 | tf_op jit(solution)/shard_map/reduce_scatter | solution.py:282
  443.7 224.8 %reduce-scatter.20.cloned.1.call-start = ((), (), s32[]{:S(2)}) async-start(), calls=%async_computation.26 | async-start | bytes 4718592 | tf_op jit(solution)/shard_map/reduce_scatter | solution.py:280
  497.7 10.7 %collective-permute-start.2 = (bf16[64,1,16,512]{3,2,0,1:T(8,128)(2,1)S(1)}, bf16[64,1,16,512]{3,2,0,1:T(8,128)(2,1)}, u32[]{:S(2)}, u32[]{:S(2)}) collective-permute-start(bf16[64,1,16,512]{3,2,0,1:T(8,128)(2,1)S(1)} %bitcast.106), channel_id=1, source_target_pairs={{0,1},{1,2},{2,3},{3,4},{4,5},{5,6},{6,7},{8,9},{9,10},{10,11},{11... | collective-permute-start | bytes 3145736 | tf_op jit(solution)/shard_map/ppermute | solution.py:15
  500.4 8.0 collective-permute-start.3
  586.3 182.1 %reduce-scatter.24.cloned.1.call-start = ((), (), s32[]{:S(2)}) async-start(), calls=%async_computation.28 | async-start | bytes 10616832 | tf_op jit(solution)/shard_map/reduce_scatter | solution.py:281
  597.8 213.5 %all-reduce.11.cloned.1.call-start = ((), (), s32[]{:S(2)}) async-start(), calls=%async_computation.41 | async-start | bytes 163840
  599.4 239.5 %reduce-scatter.48.cloned.1.call-start = ((), (), s32[]{:S(2)}) async-start(), calls=%async_computation.40 | async-start | bytes 327680
  601.4 264.2 %reduce-scatter.42.cloned.1.call-start = ((), (), s32[]{:S(2)}) async-start(), calls=%async_computation.37 | async-start | bytes 327680 | tf_op jit(solution)/shard_map/reduce_scatter | solution.py:308
  603.3 167.6 %copy-start.121 = (u32[32]{0:T(128)S(1)}, u32[32]{0:T(128)}, u32[]{:S(2)}) copy-start(u32[32]{0:T(128)} %constant.85) | copy-start | bytes 388
  603.3 168.8 %copy-start.5 = (bf16[1024,512]{1,0:T(8,128)(2,1)S(1)}, bf16[1024,512]{1,0:T(8,128)(2,1)}, u32[]{:S(2)}) copy-start(bf16[1024,512]{1,0:T(8,128)(2,1)} %copy-done.4) | copy-start | bytes 3145732
  603.3 289.4 %reduce-scatter.34.cloned.1.call-start = ((), (), s32[]{:S(2)}) async-start(), calls=%async_computation.33 | async-start | bytes 327680 | tf_op jit(solution)/shard_map/reduce_scatter | solution.py:302
  605.3 314.1 %reduce-scatter.38.cloned.1.call-start = ((), (), s32[]{:S(2)}) async-start(), calls=%async_computation.35 | async-start | bytes 327680 | tf_op jit(solution)/shard_map/reduce_scatter | solution.py:305
  607.2 339.4 %reduce-scatter.28.cloned.1.call-start = ((), (), s32[]{:S(2)}) async-start(), calls=%async_computation.30 | async-start | bytes 327680 | tf_op jit(solution)/shard_map/reduce_scatter | solution.py:296
  619.4 354.6 %reduce-scatter.22.cloned.1.call-start = ((), (), s32[]{:S(2)}) async-start(), calls=%async_computation.27 | async-start | bytes 327680 | tf_op jit(solution)/shard_map/reduce_scatter | solution.py:290
  670.3 332.3 %reduce-scatter.46.cloned.1.call-start = ((), (), s32[]{:S(2)}) async-start(), calls=%async_computation.39 | async-start | bytes 819200
  772.1 232.3 %copy-start.1 = (bf16[10,2048]{1,0:T(8,128)(2,1)S(1)}, bf16[10,2048]{1,0:T(8,128)(2,1)}, u32[]{:S(2)}) copy-start(bf16[10,2048]{1,0:T(8,128)(2,1)} %param.45) | copy-start | bytes 122884
  (105 other events, 5091.6 us)
Sparse Core Ops, SparseCore 0:
  9.6 31.8 all-gather.9
  43.2 51.9 all-gather.11
  96.8 35.5 all-gather.13
  133.9 28.7 all-gather.17
  164.2 29.0 all-gather.19
  194.7 28.8 all-gather.15
  225.2 29.4 all-gather.21
  318.2 34.8 reduce-scatter.43
  355.4 53.8 reduce-scatter.29
  411.4 49.2 reduce-scatter.39
  463.0 51.3 reduce-scatter.31
  516.6 50.5 reduce-scatter.35
  569.4 48.1 reduce-scatter.25
  620.4 48.1 reduce-scatter.19
  670.7 97.6 reduce-scatter.23
  771.7 39.4 all-reduce.10
  814.1 24.8 reduce-scatter.47
  841.5 24.0 reduce-scatter.41
  868.6 24.0 reduce-scatter.33
  895.4 24.0 reduce-scatter.37
  922.4 24.0 reduce-scatter.27
  949.9 24.0 reduce-scatter.21
  977.2 25.3 reduce-scatter.45
where the time goes:
time: 1020 us; the launch traced here: 1010 us
  waiting for transfers between devices  395 us (39%)
  blocking collectives  364 us (36%)
  matrix products  128 us (13%)
  local copies, waits for them, and re-layouts  45.6 us (4%)
  other arithmetic  43.2 us (4%)
  starting transfers between devices  18.9 us (2%)
  between operations  17.1 us (2%)
    psum x3, blocking collectives, normalize(): lax.psum((jnp.sum(field, 0), jnp.sum(field * field, 0)), ('batch', 'rows'))  126 us
    reduce_scatter x1, waiting for transfers between devices, on_device(): lax.psum_scatter(grad_wb, 'rows', scatter_dimension=0, tiled=True)  98 us
    psum x2, blocking collectives, segment_totals(): lax.psum((jnp.sum(grad, 0), jnp.sum(grad * normed, 0)), ('batch', 'rows'))  96 us
    unnamed x26, waiting for transfers between devices  88.4 us
    dot_general x11, matrix products, tdot(): lax.dot_general(left, right, (((0,), (0,)), ((), ())), preferred_element_...  49.2 us
    reduce_scatter x1, waiting for transfers between devices, on_device(): lax.psum_scatter(grad_wa, 'rows', scatter_dimension=0, tiled=True)  49.1 us
    all_gather x1, blocking collectives, on_device(): lax.all_gather(w_head, 'rows', axis=0, tiled=True)  39.7 us
    psum x1, blocking collectives, on_device(): lax.psum((jnp.sum(d_pre, 0), jnp.sum(d_pre * hat_c, 0), grad_ln_gain, gra...  38.9 us
  transfers between devices with their start and end apart: 29, of which 12 were waited for; matrix products, arithmetic and copies ran while one was open for 20% of the time, Pallas kernels for 0%

commit v1 on v0

--- a/solution.py
+++ b/solution.py
@@ -2,6 +2,7 @@
 import jax.numpy as jnp
 from jax import lax
 from jax.sharding import PartitionSpec as P
+from jax.lax import psum
 
 
 def padded(cells, sides, width):
@@ -60,7 +61,15 @@
 
 
 def normalize(field, total_count):
-    sums, squares = lax.psum((jnp.sum(field, 0), jnp.sum(field * field, 0)), ("batch", "rows"))
+
+    def _extend_axis_part(x_part, along_axis, axis_name):
+        raw_out = psum(x_part, along_axis)
+        now = psum(raw_out, axis_name)
+        return now
+
+    sums, squares = _extend_axis_part(
+        (jnp.sum(field, 0), jnp.sum(field * field, 0)), "rows", "batch"
+    )
     centre_value = sums / total_count
     inverse = lax.rsqrt(squares / total_count - centre_value * centre_value + 1e-05)
     return ((field - centre_value) * inverse, inverse)

time: 1020 us -> 984 us (0.965)
  blocking collectives: 364 us -> 327 us
    psum x3 -> x6, blocking collectives: 126 us -> 90.4 us  [the longest x3 56.6 us: _extend_axis_part(): raw_out = psum(x_part, along_axis)]
    unnamed x273 -> x277, local copies, waits for them, and re-layouts: 28.3 us -> 28.3 us
  transfers between devices with their start and end apart: 29 -> 29, of which waited for: 12 -> 12; matrix products, arithmetic and copies ran while one was open for 20% -> 21% of each run, Pallas kernels for 0% -> 0%
where the time goes in v1:
time: 984 us; the launch traced here: 973 us
  waiting for transfers between devices  394 us (40%)
  blocking collectives  327 us (33%)
  matrix products  128 us (13%)
  local copies, waits for them, and re-layouts  45.6 us (5%)
  other arithmetic  43.2 us (4%)
  starting transfers between devices  18.8 us (2%)
  between operations  16.9 us (2%)
    reduce_scatter x1, waiting for transfers between devices, on_device(): lax.psum_scatter(grad_wb, 'rows', scatter_dimension=0, tiled=True)  98 us
    psum x2, blocking collectives, segment_totals(): lax.psum((jnp.sum(grad, 0), jnp.sum(grad * normed, 0)), ('batch', 'rows'))  94 us
    unnamed x26, waiting for transfers between devices  88.4 us
    psum x3, blocking collectives, _extend_axis_part(): raw_out = psum(x_part, along_axis)  56.6 us
    dot_general x11, matrix products, tdot(): lax.dot_general(left, right, (((0,), (0,)), ((), ())), preferred_element_...  49.2 us
    reduce_scatter x1, waiting for transfers between devices, on_device(): lax.psum_scatter(grad_wa, 'rows', scatter_dimension=0, tiled=True)  49 us
    psum x1, blocking collectives, on_device(): lax.psum((jnp.sum(d_pre, 0), jnp.sum(d_pre * hat_c, 0), grad_ln_gain, gra...  38.3 us
    all_gather x1, blocking collectives, on_device(): lax.all_gather(w_head, 'rows', axis=0, tiled=True)  35.5 us
  transfers between devices with their start and end apart: 29, of which 12 were waited for; matrix products, arithmetic and copies ran while one was open for 21% of the time, Pallas kernels for 0%

profile of v1, /device:TPU:0, one launch (start us, length us, event | category | flops | bytes accessed | tf_op | source)
XLA Modules:
  0.0 973.4 jit_solution(17122837557401892970)
XLA Ops:
  11.2 6.3 all-to-all-start
  19.9 21.7 %all-gather.10.cloned.1.call-done = bf16[2048,512]{1,0:T(8,128)(2,1)} async-done(((bf16[256,512]{1,0:T(8,128)(2,1)}), bf16[2048,512]{1,0:T(8,128)(2,1)}) %all-gather.10.cloned.1.call-update) | async-done | bytes 2097168 | tf_op jit(solution)/shard_map/all_gather | solution.py:122
  41.6 5.2 fusion.49
  46.9 15.9 %all-reduce.8 = (f32[512]{0:T(512)S(1)}, f32[512]{0:T(512)S(1)}) all-reduce(f32[512]{0:T(512)S(1)} %get-tuple-element.106, f32[512]{0:T(512)S(1)} %get-tuple-element.105), channel_id=1, replica_groups=mesh['batch'=4,'rows'=8] {'rows'}, use_global_device_ids=true, to_apply=%region_4.0 | all-reduce | flops 1024 | bytes 8192 | tf_op jit(solution)/shard_map/psum | solution.py:66
  62.8 9.8 %all-reduce.11 = (f32[512]{0:T(512)S(1)}, f32[512]{0:T(512)S(1)}) all-reduce(f32[512]{0:T(512)S(1)} %get-tuple-element.180, f32[512]{0:T(512)S(1)} %get-tuple-element.181), channel_id=1, replica_groups=mesh['batch'=4,'rows'=8] {'batch'}, use_global_device_ids=true, to_apply=%region_5.0 | all-reduce | flops 1024 | bytes 8192 | tf_op jit(solution)/shard_map/psum | solution.py:67
  80.1 35.5 %all_gather.39 = bf16[4096,80]{0,1:T(8,128)(2,1)} all-gather(bf16[512,80]{0,1:T(8,128)(2,1)S(1)} %copy-done.8), channel_id=1, replica_groups=mesh['batch'=4,'rows'=8] {'rows'}, dimensions={0}, use_global_device_ids=true | all-gather | bytes 737280 | tf_op jit(solution)/shard_map/all_gather | solution.py:129
  117.3 3.7 select_maximum_fusion.2
  135.9 10.1 %fusion.48 = (f32[512]{0:T(512)S(1)}, f32[512]{0:T(512)S(1)}, f32[1024,512]{1,0:T(8,128)}) fusion(bf16[1024,4608]{1,0:T(8,128)(2,1)} %constant_dynamic-update-slice_fusion, bf16[4608,512]{1,0:T(8,128)(2,1)} %all-gather.12.cloned.1.call-done), kind=kOutput, calls=%fused_computation.239 | convolution fusion | flops 4833410048 | bytes 16257024 | tf_op jit(solution)/shard_map/dot_general | solution.py:147
  146.0 14.4 %all-reduce.7 = (f32[512]{0:T(512)S(1)}, f32[512]{0:T(512)S(1)}) all-reduce(f32[512]{0:T(512)S(1)} %get-tuple-element.104, f32[512]{0:T(512)S(1)} %get-tuple-element.103), channel_id=1, replica_groups=mesh['batch'=4,'rows'=8] {'rows'}, use_global_device_ids=true, to_apply=%region_10.11 | all-reduce | flops 1024 | bytes 8192 | tf_op jit(solution)/shard_map/psum | solution.py:66
  160.4 10.1 %all-reduce.10 = (f32[512]{0:T(512)S(1)}, f32[512]{0:T(512)S(1)}) all-reduce(f32[512]{0:T(512)S(1)} %get-tuple-element.178, f32[512]{0:T(512)S(1)} %get-tuple-element.179), channel_id=1, replica_groups=mesh['batch'=4,'rows'=8] {'batch'}, use_global_device_ids=true, to_apply=%region_11.12 | all-reduce | flops 1024 | bytes 8192 | tf_op jit(solution)/shard_map/psum | solution.py:67
  170.6 8.3 fusion.45
  178.9 26.3 %all-reduce.6 = (f32[2048]{0:T(1024)S(1)}, f32[2048]{0:T(1024)S(1)}) all-reduce(f32[2048]{0:T(1024)S(1)} %get-tuple-element.98, f32[2048]{0:T(1024)S(1)} %get-tuple-element.97), channel_id=1, replica_groups=mesh['batch'=4,'rows'=8] {'rows'}, use_global_device_ids=true, to_apply=%region_16.17 | all-reduce | flops 4096 | bytes 32768 | tf_op jit(solution)/shard_map/psum | solution.py:66
  205.2 13.9 %all-reduce.9 = (f32[2048]{0:T(1024)S(1)}, f32[2048]{0:T(1024)S(1)}) all-reduce(f32[2048]{0:T(1024)S(1)} %get-tuple-element.176, f32[2048]{0:T(1024)S(1)} %get-tuple-element.177), channel_id=1, replica_groups=mesh['batch'=4,'rows'=8] {'batch'}, use_global_device_ids=true, to_apply=%region_17.18 | all-reduce | flops 4096 | bytes 32768 | tf_op jit(solution)/shard_map/psum | solution.py:67
  219.6 10.3 %fusion.6 = bf16[8,8,2048]{2,1,0:T(8,128)(2,1)} fusion(bf16[1024,2048]{1,0:T(8,128)(2,1)} %bitcast.110, f32[2048]{0:T(1024)S(1)} %copy-done.118, f32[2048]{0:T(1024)S(1)} %get-tuple-element.203, f32[1024,2048]{1,0:T(8,128)} %get-tuple-element.213, f32[2048]{0:T(1024)S(1)} %get-tuple-element.204, f32[2048]{0:T(1024)S(1)} %copy-done.20, ...), kind=kOutput, calls=%fused_computation.27 | convolution fusion | flops 297140224 | bytes 12892160 | tf_op jit(solution)/shard_map/dot_general | solution.py:174
  229.9 3.4 all-to-all-start.1
  235.3 21.5 %all-gather = bf16[8,10,512]{2,1,0:T(8,128)(2,1)S(1)} all-gather(bf16[1,10,512]{2,1,0:T(8,128)(2,1)S(1)} %fusion.14), channel_id=1, replica_groups=mesh['batch'=4,'rows'=8] {'rows'}, dimensions={0}, use_global_device_ids=true | all-gather | bytes 92160 | tf_op jit(solution)/shard_map/all_gather | solution.py:192
  258.9 14.0 %all-gather.1 = bf16[8,10,512]{2,1,0:T(8,128)(2,1)S(1)} all-gather(bf16[1,10,512]{2,1,0:T(8,128)(2,1)S(1)} %fusion.15), channel_id=1, replica_groups=mesh['batch'=4,'rows'=8] {'rows'}, dimensions={0}, use_global_device_ids=true | all-gather | bytes 92160 | tf_op jit(solution)/shard_map/all_gather | solution.py:193
  279.4 2.8 convert_reduce_fusion
  286.8 3.2 multiply_reduce_fusion.6
  293.4 4.2 fusion.20
  298.1 16.5 %all_to_all.24 = bf16[8,10,1024]{2,1,0:T(8,128)(2,1)S(1)} all-to-all(bf16[8,10,1024]{2,1,0:T(8,128)(2,1)S(1)} %reshape.231), channel_id=1, replica_groups=mesh['batch'=4,'rows'=8] {'rows'}, dimensions={0} | all-to-all | bytes 327680 | tf_op jit(solution)/shard_map/all_to_all | solution.py:33
  320.7 3.0 fusion.4
  324.5 16.6 %all_to_all.25 = bf16[8,8,2048]{2,1,0:T(8,128)(2,1)S(1)} all-to-all(bf16[8,8,2048]{2,1,0:T(8,128)(2,1)S(1)} %bitcast_select_fusion), channel_id=1, replica_groups=mesh['batch'=4,'rows'=8] {'rows'}, dimensions={0} | all-to-all | bytes 524288 | tf_op jit(solution)/shard_map/all_to_all | solution.py:251
  341.5 14.8 %fusion.44 = (f32[2048]{0:T(1024)S(1)}, f32[2048]{0:T(1024)S(1)}, f32[1024,2048]{1,0:T(8,128)}) fusion(f32[2048]{0:T(1024)S(1)} %get-tuple-element.203, f32[1024,2048]{1,0:T(8,128)} %get-tuple-element.213, f32[2048]{0:T(1024)S(1)} %get-tuple-element.204, bf16[1024,2048]{1,0:T(8,128)(2,1)} %bitcast.111, f32[2048]{0:T(1024)} %param.41, ...), kind=kOutput, calls=%fused_computation.235 | convolution fusion | flops 309587968 | bytes 21297152 | tf_op jit(solution)/shard_map/dot_general | solution.py:47
  356.3 38.3 %all-reduce.5 = (f32[2048]{0:T(1024)S(1)}, f32[2048]{0:T(1024)S(1)}) all-reduce(f32[2048]{0:T(1024)S(1)} %get-tuple-element.96, f32[2048]{0:T(1024)S(1)} %get-tuple-element.95), channel_id=1, replica_groups=mesh['batch'=4,'rows'=8] {'batch','rows'}, use_global_device_ids=true, to_apply=%region_28.29 | all-reduce | flops 4096 | bytes 32768 | tf_op jit(solution)/shard_map/psum | solution.py:254
  394.6 7.4 multiply_convert_fusion
  404.1 4.5 fusion.42
  409.1 8.1 fusion.47
  417.2 41.4 %all-reduce.4 = (f32[512]{0:T(512)S(1)}, f32[512]{0:T(512)S(1)}) all-reduce(f32[512]{0:T(512)S(1)} %get-tuple-element.102, f32[512]{0:T(512)S(1)} %get-tuple-element.101), channel_id=1, replica_groups=mesh['batch'=4,'rows'=8] {'batch','rows'}, use_global_device_ids=true, to_apply=%region_32.33 | all-reduce | flops 1024 | bytes 8192 | tf_op jit(solution)/shard_map/psum | solution.py:79
  458.6 2.8 multiply_convert_fusion.8
  465.4 6.7 copy.62
  472.1 3.6 select_maximum_fusion
  481.7 7.1 fusion.46
  488.9 52.6 %all-reduce.3 = (f32[512]{0:T(512)S(1)}, f32[512]{0:T(512)S(1)}, f32[512]{0:T(512)}, f32[512]{0:T(512)}, f32[80]{0:T(128)}) all-reduce(f32[512]{0:T(512)S(1)} %get-tuple-element.100, f32[512]{0:T(512)S(1)} %get-tuple-element.99, f32[512]{0:T(512)S(1)} %copy-done.28, ...), channel_id=1, replica_groups=mesh['batch'=4,'rows'=8] {'batch','rows'}, use_global_device_ids=true, to_apply=%region_36.37 | all-reduce | flops 2128 | bytes 17024 | tf_op jit(solution)/shard_map/psum | solution.py:79
  544.9 4.4 convolution_bitcast_fusion.2
  549.4 11.4 %fusion.57 = f32[4608,512]{1,0:T(8,128)} fusion(bf16[1024,4608]{1,0:T(8,128)(2,1)} %constant_dynamic-update-slice_fusion, bf16[1024,512]{1,0:T(8,128)(2,1)S(1)} %multiply_convert_fusion.8), kind=kOutput, calls=%fused_computation.247 | convolution fusion | flops 4831838208 | bytes 19922944 | tf_op jit(solution)/shard_map/dot_general | solution.py:47
  570.3 9.7 reduce-scatter.26.cloned.1.call-done
  581.8 49.0 %reduce-scatter.20.cloned.1.call-done = f32[256,512]{0,1:T(8,128)} async-done(((f32[2048,512]{0,1:T(8,128)}), f32[256,512]{0,1:T(8,128)}) %reduce-scatter.20.cloned.1.call-update) | async-done | bytes 524304 | tf_op jit(solution)/shard_map/reduce_scatter | solution.py:289
  632.7 98.0 %reduce-scatter.24.cloned.1.call-done = f32[576,512]{1,0:T(8,128)} async-done(((f32[4608,512]{1,0:T(8,128)}), f32[576,512]{1,0:T(8,128)}) %reduce-scatter.24.cloned.1.call-update) | async-done | bytes 1179664 | tf_op jit(solution)/shard_map/reduce_scatter | solution.py:290
  734.5 8.5 add_convert_fusion
  743.0 30.5 %all-reduce.14.cloned.1.call-done = bf16[512,80]{0,1:T(8,128)(2,1)} async-done(((bf16[512,80]{0,1:T(8,128)(2,1)}), bf16[512,80]{0,1:T(8,128)(2,1)}) %all-reduce.14.cloned.1.call-update) | async-done | bytes 81936
  774.9 26.3 %reduce-scatter.48.cloned.1.call-done = bf16[128,256]{1,0:T(8,128)(2,1)} async-done(((bf16[512,256]{1,0:T(8,128)(2,1)}), bf16[128,256]{1,0:T(8,128)(2,1)}) %reduce-scatter.48.cloned.1.call-update) | async-done | bytes 65552
  802.9 25.1 %reduce-scatter.42.cloned.1.call-done = bf16[64,512]{1,0:T(8,128)(2,1)} async-done(((bf16[64,2048]{1,0:T(8,128)(2,1)}), bf16[64,512]{1,0:T(8,128)(2,1)}) %reduce-scatter.42.cloned.1.call-update) | async-done | bytes 65552 | tf_op jit(solution)/shard_map/reduce_scatter | solution.py:317
  829.5 25.6 %reduce-scatter.34.cloned.1.call-done = bf16[256,128]{0,1:T(8,128)(2,1)} async-done(((bf16[256,512]{0,1:T(8,128)(2,1)}), bf16[256,128]{0,1:T(8,128)(2,1)}) %reduce-scatter.34.cloned.1.call-update) | async-done | bytes 65552 | tf_op jit(solution)/shard_map/reduce_scatter | solution.py:311
  856.7 25.1 %reduce-scatter.38.cloned.1.call-done = bf16[256,128]{0,1:T(8,128)(2,1)} async-done(((bf16[256,512]{0,1:T(8,128)(2,1)}), bf16[256,128]{0,1:T(8,128)(2,1)}) %reduce-scatter.38.cloned.1.call-update) | async-done | bytes 65552 | tf_op jit(solution)/shard_map/reduce_scatter | solution.py:314
  883.4 25.5 %reduce-scatter.28.cloned.1.call-done = bf16[64,512]{1,0:T(8,128)(2,1)} async-done(((bf16[64,2048]{1,0:T(8,128)(2,1)}), bf16[64,512]{1,0:T(8,128)(2,1)}) %reduce-scatter.28.cloned.1.call-update) | async-done | bytes 65552 | tf_op jit(solution)/shard_map/reduce_scatter | solution.py:305
  910.4 26.0 %reduce-scatter.22.cloned.1.call-done = bf16[256,128]{0,1:T(8,128)(2,1)} async-done(((bf16[256,512]{0,1:T(8,128)(2,1)}), bf16[256,128]{0,1:T(8,128)(2,1)}) %reduce-scatter.22.cloned.1.call-update) | async-done | bytes 65552 | tf_op jit(solution)/shard_map/reduce_scatter | solution.py:299
  938.0 27.0 %reduce-scatter.46.cloned.1.call-done = bf16[128,576]{1,0:T(8,128)(2,1)} async-done(((bf16[512,576]{1,0:T(8,128)(2,1)}), bf16[128,576]{1,0:T(8,128)(2,1)}) %reduce-scatter.46.cloned.1.call-update) | async-done | bytes 147472
  (419 shorter events, 100.3 us)
Async XLA Ops:
  7.2 226.2 %copy-start = (bf16[10,2048]{1,0:T(8,128)(2,1)S(1)}, bf16[10,2048]{1,0:T(8,128)(2,1)}, u32[]{:S(2)}) copy-start(bf16[10,2048]{1,0:T(8,128)(2,1)} %param.45) | copy-start | bytes 122884
  7.2 34.4 %all-gather.10.cloned.1.call-start = ((), (), s32[]{:S(2)}) async-start(), calls=%async_computation.19 | async-start | bytes 2359296 | tf_op jit(solution)/shard_map/all_gather | solution.py:122
  7.9 128.0 %all-gather.12.cloned.1.call-start = ((), (), s32[]{:S(2)}) async-start(), calls=%async_computation.20 | async-start | bytes 5308416 | tf_op jit(solution)/shard_map/all_gather | solution.py:123
  8.7 161.8 %all-gather.14.cloned.1.call-start = ((), (), s32[]{:S(2)}) async-start(), calls=%async_computation.21 | async-start | bytes 2359296 | tf_op jit(solution)/shard_map/all_gather | solution.py:124
  9.4 223.9 %all-gather.18.cloned.1.call-start = ((), (), s32[]{:S(2)}) async-start(), calls=%async_computation.23 | async-start | bytes 2359296 | tf_op jit(solution)/shard_map/all_gather | solution.py:126
  10.0 246.9 %all-gather.20.cloned.1.call-start = ((), (), s32[]{:S(2)}) async-start(), calls=%async_computation.24 | async-start | bytes 2359296 | tf_op jit(solution)/shard_map/all_gather | solution.py:127
  10.6 263.6 %all-gather.16.cloned.1.call-start = ((), (), s32[]{:S(2)}) async-start(), calls=%async_computation.22 | async-start | bytes 2359296 | tf_op jit(solution)/shard_map/all_gather | solution.py:125
  11.2 104.9 %all-to-all-start = ((s32[8,1,8]{2,1,0:T(1,128)}), s32[8,1,8]{2,1,0:T(1,128)S(1)}, u32[]{:S(2)}, u32[]{:S(2)}) async-start(s32[8,1,8]{2,1,0:T(1,128)} %bitcast.138), calls=%async_computation | async-start | bytes 8192 | tf_op jit(solution)/shard_map/all_to_all | solution.py:180
  17.5 259.5 %all-gather.22.cloned.1.call-start = ((), (), s32[]{:S(2)}) async-start(), calls=%async_computation.25 | async-start | bytes 2359296 | tf_op jit(solution)/shard_map/all_gather | solution.py:128
  73.2 44.1 %collective-permute-start = (bf16[64,1,16,512]{3,2,0,1:T(8,128)(2,1)S(1)}, bf16[64,1,16,512]{3,2,0,1:T(8,128)(2,1)}, u32[]{:S(2)}, u32[]{:S(2)}) collective-permute-start(bf16[64,1,16,512]{3,2,0,1:T(8,128)(2,1)S(1)} %bitcast.117), channel_id=1, source_target_pairs={{0,1},{1,2},{2,3},{3,4},{4,5},{5,6},{6,7},{8,9},{9,10},{10,11},{11... | collective-permute-start | bytes 3145736 | tf_op jit(solution)/shard_map/ppermute | solution.py:16
  75.5 41.8 %collective-permute-start.1 = (bf16[64,1,16,512]{3,2,0,1:T(8,128)(2,1)S(1)}, bf16[64,1,16,512]{3,2,0,1:T(8,128)(2,1)}, u32[]{:S(2)}, u32[]{:S(2)}) collective-permute-start(bf16[64,1,16,512]{3,2,0,1:T(8,128)(2,1)S(1)} %bitcast.118), channel_id=1, source_target_pairs={{1,0},{2,1},{3,2},{4,3},{5,4},{6,5},{7,6},{9,8},{10,9},{11,10},{12... | collective-permute-start | bytes 3145736 | tf_op jit(solution)/shard_map/ppermute | solution.py:18
  77.4 141.7 %copy-start.35 = (s32[64]{0:T(128)}, s32[64]{0:T(128)S(1)}, u32[]{:S(2)}) copy-start(s32[64]{0:T(128)S(1)} %get-tuple-element.149) | copy-start | bytes 772
  77.4 141.7 %copy-start.37 = (s32[64]{0:T(128)}, s32[64]{0:T(128)S(1)}, u32[]{:S(2)}) copy-start(s32[64]{0:T(128)S(1)} %get-tuple-element.150) | copy-start | bytes 772
  77.4 141.7 %copy-start.39 = (s32[64]{0:T(128)}, s32[64]{0:T(128)S(1)}, u32[]{:S(2)}) copy-start(s32[64]{0:T(128)S(1)} %get-tuple-element.151) | copy-start | bytes 772
  77.5 141.7 %copy-start.41 = (s32[64]{0:T(128)}, s32[64]{0:T(128)S(1)}, u32[]{:S(2)}) copy-start(s32[64]{0:T(128)S(1)} %get-tuple-element.152) | copy-start | bytes 772
  77.5 141.7 %copy-start.43 = (s32[64]{0:T(128)}, s32[64]{0:T(128)S(1)}, u32[]{:S(2)}) copy-start(s32[64]{0:T(128)S(1)} %get-tuple-element.153) | copy-start | bytes 772
  77.5 141.7 %copy-start.45 = (s32[64]{0:T(128)}, s32[64]{0:T(128)S(1)}, u32[]{:S(2)}) copy-start(s32[64]{0:T(128)S(1)} %get-tuple-element.154) | copy-start | bytes 772
  77.5 141.7 %copy-start.47 = (s32[64]{0:T(128)}, s32[64]{0:T(128)S(1)}, u32[]{:S(2)}) copy-start(s32[64]{0:T(128)S(1)} %get-tuple-element.155) | copy-start | bytes 772
  77.5 141.7 %copy-start.49 = (s32[64]{0:T(128)}, s32[64]{0:T(128)S(1)}, u32[]{:S(2)}) copy-start(s32[64]{0:T(128)S(1)} %get-tuple-element.156) | copy-start | bytes 772
  77.5 141.7 %copy-start.51 = (s32[64]{0:T(128)}, s32[64]{0:T(128)S(1)}, u32[]{:S(2)}) copy-start(s32[64]{0:T(128)S(1)} %get-tuple-element.157) | copy-start | bytes 772
  78.7 140.5 %copy-start.83 = (s32[64]{0:T(128)}, s32[64]{0:T(128)S(1)}, u32[]{:S(2)}) copy-start(s32[64]{0:T(128)S(1)} %get-tuple-element.116) | copy-start | bytes 772
  78.7 140.5 %copy-start.85 = (s32[64]{0:T(128)}, s32[64]{0:T(128)S(1)}, u32[]{:S(2)}) copy-start(s32[64]{0:T(128)S(1)} %get-tuple-element.117) | copy-start | bytes 772
  78.7 140.5 %copy-start.87 = (s32[64]{0:T(128)}, s32[64]{0:T(128)S(1)}, u32[]{:S(2)}) copy-start(s32[64]{0:T(128)S(1)} %get-tuple-element.118) | copy-start | bytes 772
  78.8 140.5 %copy-start.89 = (s32[64]{0:T(128)}, s32[64]{0:T(128)S(1)}, u32[]{:S(2)}) copy-start(s32[64]{0:T(128)S(1)} %get-tuple-element.119) | copy-start | bytes 772
  78.8 140.5 %copy-start.91 = (s32[64]{0:T(128)}, s32[64]{0:T(128)S(1)}, u32[]{:S(2)}) copy-start(s32[64]{0:T(128)S(1)} %get-tuple-element.120) | copy-start | bytes 772
  78.8 140.5 %copy-start.93 = (s32[64]{0:T(128)}, s32[64]{0:T(128)S(1)}, u32[]{:S(2)}) copy-start(s32[64]{0:T(128)S(1)} %get-tuple-element.121) | copy-start | bytes 772
  229.9 43.0 %all-to-all-start.1 = ((bf16[8,8,2048]{2,1,0:T(8,128)(2,1)}), bf16[8,8,2048]{2,1,0:T(8,128)(2,1)S(1)}, u32[]{:S(2)}, u32[]{:S(2)}) async-start(bf16[8,8,2048]{2,1,0:T(8,128)(2,1)} %fusion.6), calls=%async_computation.1 | async-start | bytes 524288 | tf_op jit(solution)/shard_map/all_to_all | solution.py:179
  233.3 327.6 %reduce-scatter.44.cloned.1.call-start = ((), (), s32[]{:S(2)}) async-start(), calls=%async_computation.38 | async-start | bytes 1474560 | tf_op jit(solution)/shard_map/reduce_scatter | solution.py:296
  283.7 278.9 %reduce-scatter.30.cloned.1.call-start = ((), (), s32[]{:S(2)}) async-start(), calls=%async_computation.31 | async-start | bytes 4718592 | tf_op jit(solution)/shard_map/reduce_scatter | solution.py:292
  293.4 271.2 %reduce-scatter.40.cloned.1.call-start = ((), (), s32[]{:S(2)}) async-start(), calls=%async_computation.36 | async-start | bytes 4718592 | tf_op jit(solution)/shard_map/reduce_scatter | solution.py:295
  297.6 268.8 %reduce-scatter.32.cloned.1.call-start = ((), (), s32[]{:S(2)}) async-start(), calls=%async_computation.32 | async-start | bytes 4718592 | tf_op jit(solution)/shard_map/reduce_scatter | solution.py:293
  317.4 251.1 %reduce-scatter.36.cloned.1.call-start = ((), (), s32[]{:S(2)}) async-start(), calls=%async_computation.34 | async-start | bytes 4718592 | tf_op jit(solution)/shard_map/reduce_scatter | solution.py:294
  320.5 259.5 %reduce-scatter.26.cloned.1.call-start = ((), (), s32[]{:S(2)}) async-start(), calls=%async_computation.29 | async-start | bytes 4718592 | tf_op jit(solution)/shard_map/reduce_scatter | solution.py:291
  408.6 222.2 %reduce-scatter.20.cloned.1.call-start = ((), (), s32[]{:S(2)}) async-start(), calls=%async_computation.26 | async-start | bytes 4718592 | tf_op jit(solution)/shard_map/reduce_scatter | solution.py:289
  461.4 10.7 %collective-permute-start.2 = (bf16[64,1,16,512]{3,2,0,1:T(8,128)(2,1)S(1)}, bf16[64,1,16,512]{3,2,0,1:T(8,128)(2,1)}, u32[]{:S(2)}, u32[]{:S(2)}) collective-permute-start(bf16[64,1,16,512]{3,2,0,1:T(8,128)(2,1)S(1)} %bitcast.106), channel_id=1, source_target_pairs={{0,1},{1,2},{2,3},{3,4},{4,5},{5,6},{6,7},{8,9},{9,10},{10,11},{11... | collective-permute-start | bytes 3145736 | tf_op jit(solution)/shard_map/ppermute | solution.py:16
  464.1 8.0 collective-permute-start.3
  549.3 181.4 %reduce-scatter.24.cloned.1.call-start = ((), (), s32[]{:S(2)}) async-start(), calls=%async_computation.28 | async-start | bytes 10616832 | tf_op jit(solution)/shard_map/reduce_scatter | solution.py:290
  560.8 212.7 %all-reduce.14.cloned.1.call-start = ((), (), s32[]{:S(2)}) async-start(), calls=%async_computation.41 | async-start | bytes 163840
  562.5 238.7 %reduce-scatter.48.cloned.1.call-start = ((), (), s32[]{:S(2)}) async-start(), calls=%async_computation.40 | async-start | bytes 327680
  564.5 263.5 %reduce-scatter.42.cloned.1.call-start = ((), (), s32[]{:S(2)}) async-start(), calls=%async_computation.37 | async-start | bytes 327680 | tf_op jit(solution)/shard_map/reduce_scatter | solution.py:317
  566.4 166.8 %copy-start.123 = (u32[32]{0:T(128)S(1)}, u32[32]{0:T(128)}, u32[]{:S(2)}) copy-start(u32[32]{0:T(128)} %constant.85) | copy-start | bytes 388
  566.4 168.1 %copy-start.5 = (bf16[1024,512]{1,0:T(8,128)(2,1)S(1)}, bf16[1024,512]{1,0:T(8,128)(2,1)}, u32[]{:S(2)}) copy-start(bf16[1024,512]{1,0:T(8,128)(2,1)} %copy-done.4) | copy-start | bytes 3145732
  566.4 288.7 %reduce-scatter.34.cloned.1.call-start = ((), (), s32[]{:S(2)}) async-start(), calls=%async_computation.33 | async-start | bytes 327680 | tf_op jit(solution)/shard_map/reduce_scatter | solution.py:311
  568.4 313.4 %reduce-scatter.38.cloned.1.call-start = ((), (), s32[]{:S(2)}) async-start(), calls=%async_computation.35 | async-start | bytes 327680 | tf_op jit(solution)/shard_map/reduce_scatter | solution.py:314
  570.3 338.6 %reduce-scatter.28.cloned.1.call-start = ((), (), s32[]{:S(2)}) async-start(), calls=%async_computation.30 | async-start | bytes 327680 | tf_op jit(solution)/shard_map/reduce_scatter | solution.py:305
  581.8 354.6 %reduce-scatter.22.cloned.1.call-start = ((), (), s32[]{:S(2)}) async-start(), calls=%async_computation.27 | async-start | bytes 327680 | tf_op jit(solution)/shard_map/reduce_scatter | solution.py:299
  632.7 332.3 %reduce-scatter.46.cloned.1.call-start = ((), (), s32[]{:S(2)}) async-start(), calls=%async_computation.39 | async-start | bytes 819200
  734.5 232.3 %copy-start.1 = (bf16[10,2048]{1,0:T(8,128)(2,1)S(1)}, bf16[10,2048]{1,0:T(8,128)(2,1)}, u32[]{:S(2)}) copy-start(bf16[10,2048]{1,0:T(8,128)(2,1)} %param.45) | copy-start | bytes 122884
  (107 other events, 4540.1 us)
Sparse Core Ops, SparseCore 0:
  9.6 31.8 all-gather.9
  43.2 55.0 all-gather.11
  99.9 33.1 all-gather.13
  134.6 28.8 all-gather.17
  165.0 28.9 all-gather.19
  195.4 28.6 all-gather.15
  225.7 35.8 all-gather.21
  283.8 32.4 reduce-scatter.43
  318.6 54.1 reduce-scatter.29
  375.0 49.0 reduce-scatter.39
  426.4 51.2 reduce-scatter.31
  479.9 49.4 reduce-scatter.35
  531.7 48.2 reduce-scatter.25
  582.7 48.1 reduce-scatter.19
  633.0 97.6 reduce-scatter.23
  734.1 39.4 all-reduce.13
  776.4 24.8 reduce-scatter.47
  803.8 24.0 reduce-scatter.41
  831.0 24.0 reduce-scatter.33
  857.7 24.0 reduce-scatter.37
  884.8 24.0 reduce-scatter.27
  912.2 24.0 reduce-scatter.21
  939.5 25.3 reduce-scatter.45
